TPU v7x, 32 devices: a whole 2x2x4 slice. The times are simulated.
32 devices in a mesh: probe: 4 (over z), gx: 4 (over x, core), gy: 2 (over y).
Axes of the slice: x: 2, y: 2, z: 4, core: 2. Of those that a mesh axis runs over, the one named last changes fastest.
Arguments:
- wave_prev: float32 [4, 128, 256, 256], P('probe', 'gx', 'gy'), may hold values from -6 to 6
- wave_cur: float32 [4, 128, 256, 256], P('probe', 'gx', 'gy'), may hold values from -6 to 6
- courant: float32 [128, 256, 256], P('gx', 'gy'), may hold values from 0.02 to 0.16
- perturb: float32 [4, 128, 256, 256], P('probe', 'gx', 'gy'), may hold values from -4 to 4
- snapshots: bfloat16 [8, 128, 256, 256], P('probe', 'gx', 'gy'), may hold values from -6 to 6
- step_slots: int32 [6], replicated, may hold values from 0 to 7, as said below
- precond: float32 [256], replicated, may hold values from 0.5 to 2
- probe_ids: int32 [4], P('probe'), may hold values from 0 to 255, as said below
Outputs:
- earlier: float32 [4, 128, 256, 256], P('probe', 'gx', 'gy')
- latest: float32 [4, 128, 256, 256], P('probe', 'gx', 'gy')
Inputs may be any that keep to these rules, and one draw needn't show every extreme that they name: `step_slots`: distinct slots; 0 and 7 are always among them. `probe_ids`: distinct indices; 0 and 255 are always among them.
All inputs are finite; a program needn't handle non-finite values.
Results may differ from a plain program's by a relative error of at most 0.0003.
Values may be sent and summed in bfloat16 or wider, within the bound.
A program may use at most 192 MiB of HBM per device.

v0:
```python
import jax
import jax.numpy as jnp
from jax import lax
from jax.sharding import PartitionSpec as P

STEPS = 4
COEFFS = (-205.0 / 72.0, 8.0 / 5.0, -1.0 / 5.0, 8.0 / 315.0, -1.0 / 560.0)


def spread(value, axis, source):
    kept = jnp.where(lax.axis_index(axis) == source, value, 0).astype(value.dtype)
    return lax.psum(kept, axis)


def with_halo(block, sides, width):
    for axis, dim in sides:
        count = lax.axis_size(axis)
        forward = [(i, i + 1) for i in range(count - 1)]
        backward = [(target, source) for source, target in forward]
        low = lax.ppermute(
            lax.slice_in_dim(block, block.shape[dim] - width, None, axis=dim), axis, forward
        )
        high = lax.ppermute(lax.slice_in_dim(block, 0, width, axis=dim), axis, backward)
        block = jnp.concatenate([low, block, high], axis=dim)
    return block


def stencil(padded, field):
    extent_x = field.shape[1]
    extent_y = field.shape[2]
    extent_z = field.shape[3]
    total = 3.0 * COEFFS[0] * field
    for offset in range(1, 5):
        factor = COEFFS[offset]
        along = padded[:, 4 + offset : 4 + offset + extent_x, 4 : 4 + extent_y, 4 : 4 + extent_z]
        along = (
            along
            + padded[:, 4 - offset : 4 - offset + extent_x, 4 : 4 + extent_y, 4 : 4 + extent_z]
        )
        along = (
            along
            + padded[:, 4 : 4 + extent_x, 4 + offset : 4 + offset + extent_y, 4 : 4 + extent_z]
        )
        along = (
            along
            + padded[:, 4 : 4 + extent_x, 4 - offset : 4 - offset + extent_y, 4 : 4 + extent_z]
        )
        along = (
            along
            + padded[:, 4 : 4 + extent_x, 4 : 4 + extent_y, 4 + offset : 4 + offset + extent_z]
        )
        along = (
            along
            + padded[:, 4 : 4 + extent_x, 4 : 4 + extent_y, 4 - offset : 4 - offset + extent_z]
        )
        total = total + factor * along
    return total


def shards(wave_prev, wave_cur, courant, perturb, snapshots, step_slots, precond, probe_ids):
    table = jnp.arange(precond.shape[0], dtype=jnp.int32)
    matches = (probe_ids[:, None] == table[None, :]).astype(jnp.float32)
    weight = jnp.sum(matches * precond[None, :], axis=1)
    scaled = weight[:, None, None, None] * perturb
    slot_dev = snapshots.shape[0]

    def fetch(position):
        wanted = step_slots[position]
        owner = wanted // slot_dev
        holding = lax.dynamic_index_in_dim(snapshots, wanted % slot_dev, 0, keepdims=False)
        return spread(holding, "probe", owner).astype(jnp.float32)

    frames = [fetch(0), fetch(1)]
    previous = wave_prev
    current = wave_cur
    for index in range(STEPS):
        frames.append(fetch(index + 2))
        source = frames[index + 2] - 2.0 * frames[index + 1] + frames[index]
        widened = with_halo(current, (("gx", 1), ("gy", 2)), 4)
        padded = jnp.pad(widened, ((0, 0), (0, 0), (0, 0), (4, 4)))
        laplace = stencil(padded, current)
        following = 2.0 * current - previous + courant[None] * laplace - scaled * source[None]
        previous = current
        current = following
    return (previous, current)


def solution(mesh):
    placed = (
        P("probe", "gx", "gy", None),
        P("probe", "gx", "gy", None),
        P("gx", "gy", None),
        P("probe", "gx", "gy", None),
        P("probe", "gx", "gy", None),
        P(),
        P(),
        P("probe"),
    )
    return jax.shard_map(
        shards,
        mesh=mesh,
        in_specs=placed,
        out_specs=(P("probe", "gx", "gy", None), P("probe", "gx", "gy", None)),
        check_vma=False,
    )
```

profile of v0, /device:TPU:6, one launch (start us, length us, event | category | flops | bytes accessed | tf_op | source)
XLA Modules:
  0.0 834.7 jit_solution(7365499890127130381)
XLA Ops:
  23.9 9.7 %select_bitcast_fusion = (bf16[32,128,256]{2,1,0:T(8,128)(2,1)}, bf16[32,128,256]{2,1,0:T(8,128)(2,1)}, bf16[32,128,256]{2,1,0:T(8,128)(2,1)}, bf16[32,128,256]{...) fusion(bf16[2,32,128,256]{3,2,1,0:T(8,128)(2,1)} %param.12, s32[]{:T(128)S(6)} %select_n.154, ...), kind=kLoop, calls=%fused_computation.247 | loop fusion | flops 6291456 | bytes 25165854 | tf_op jit(solution)/shard_map/jit(_where)/select_n | solution.py:11
  36.8 3.6 collective-permute-start
  40.5 4.9 collective-permute-done.1
  46.3 7.0 constant_dynamic-update-slice_fusion.1
  54.2 2.4 collective-permute-start.2
  59.5 4.4 collective-permute-done.3
  63.9 5.8 select_maximum_fusion.12
  69.6 394.8 %all-reduce.7.cloned.1.call-done = (bf16[32,128,256]{2,1,0:T(8,128)(2,1)}, bf16[32,128,256]{2,1,0:T(8,128)(2,1)}, bf16[32,128,256]{2,1,0:T(8,128)(2,1)}, bf16[32...) async-done(((bf16[32,128,256]{2,1,0:T(8,128)(2,1)}, bf16[32,128,256]{2,1,0:T(8,128)(2,1)}, bf16[32,128,256]{2,1,0:T(8,128)(2,1)}, ...) | async-done | bytes 12582928 | tf_op jit(solution)/shard_map/psum | solution.py:12
  464.5 55.3 %fusion.103 = f32[1,32,128,256]{3,2,1,0:T(8,128)S(1)} fusion(f32[1,40,128,256]{3,2,1,0:T(8,128)} %copy-done.3, bf16[32,128,256]{2,1,0:T(8,128)(2,1)} %get-tuple-element.2, bf16[32,128,256]{2,1,0:T(8,128)(2,1)} %get-tuple-element.3, f32[1,40,4,256]{3,2,1,0:T(4,128)S(1)} %collective-permute-done.3, f32[1,40,4,256]{3,2,1,0:T(4,128)S(1)} %collective-permute-done.2, ...), kind=kLoop, calls=%fused_computation.183 | loop fusion | flops 52428800 | bytes 99942400 | tf_op jit(solution)/shard_map/sub | solution.py:82
  521.8 2.4 collective-permute-start.5
  524.2 4.2 collective-permute-done.4
  528.4 3.8 collective-permute-done.5
  532.3 2.5 collective-permute-start.6
  537.6 4.4 collective-permute-done.7
  542.0 4.9 pad_maximum_fusion
  546.9 8.7 %select_maximum_fusion.8 = f32[1,40,136,264]{3,2,1,0:T(8,128)} fusion(f32[1,40,4,256]{3,2,1,0:T(4,128)S(1)} %collective-permute-done.6, f32[1,40,4,256]{3,2,1,0:T(4,128)S(1)} %collective-permute-done.7, f32[1,4,128,256]{3,2,1,0:T(8,128)S(1)} %collective-permute-done.4, f32[1,32,128,256]{3,2,1,0:T(8,128)S(1)} %fusion.103, ...), kind=kLoop, calls=%fused_computation.16 | loop fusion | flops 17233920 | bytes 11315200 | tf_op jit(solution)/shard_map/concatenate | solution.py:24
  555.6 66.3 %fusion.74 = f32[1,32,128,256]{3,2,1,0:T(8,128)} fusion(f32[1,32,128,256]{3,2,1,0:T(8,128)} %copy-done, bf16[32,128,256]{2,1,0:T(8,128)(2,1)} %get-tuple-element.2, bf16[32,128,256]{2,1,0:T(8,128)(2,1)S(1)} %copy-done.4, bf16[32,128,256]{2,1,0:T(8,128)(2,1)} %get-tuple-element.5, f32[1,4,128,256]{3,2,1,0:T(8,128)S(1)} %collective-permute-done.5, ...), kind=kLoop, calls=%fused_computation.154 | loop fusion | flops 52428800 | bytes 95420416 | tf_op jit(solution)/shard_map/sub | solution.py:82
  623.3 2.1 collective-permute-start.8
  625.4 2.4 collective-permute-start.9
  627.8 4.2 collective-permute-done.8
  632.1 3.8 collective-permute-done.9
  641.3 4.4 collective-permute-done.11
  645.7 4.9 pad_maximum_fusion.1
  650.6 8.7 %select_maximum_fusion.4 = f32[1,40,136,264]{3,2,1,0:T(8,128)} fusion(f32[1,40,4,256]{3,2,1,0:T(4,128)S(1)} %collective-permute-done.10, f32[1,40,4,256]{3,2,1,0:T(4,128)S(1)} %collective-permute-done.11, f32[1,4,128,256]{3,2,1,0:T(8,128)S(1)} %collective-permute-done.8, f32[1,32,128,256]{3,2,1,0:T(8,128)S(1)} %copy-done.1, ...), kind=kLoop, calls=%fused_computation.12 | loop fusion | flops 17233920 | bytes 11315200 | tf_op jit(solution)/shard_map/concatenate | solution.py:24
  659.2 65.8 %fusion.43 = f32[1,32,128,256]{3,2,1,0:T(8,128)} fusion(f32[1,32,128,256]{3,2,1,0:T(8,128)} %fusion.74, bf16[32,128,256]{2,1,0:T(8,128)(2,1)S(1)} %copy-done.4, bf16[32,128,256]{2,1,0:T(8,128)(2,1)} %get-tuple-element.6, bf16[32,128,256]{2,1,0:T(8,128)(2,1)} %get-tuple-element.5, f32[1,4,128,256]{3,2,1,0:T(8,128)S(1)} %collective-permute-done.9, ...), kind=kLoop, calls=%fused_computation.123 | loop fusion | flops 52428800 | bytes 95420416 | tf_op jit(solution)/shard_map/sub | solution.py:82
  728.5 2.4 collective-permute-start.13
  731.0 4.2 collective-permute-done.12
  735.2 3.8 collective-permute-done.13
  744.4 4.4 collective-permute-done.15
  748.8 4.9 pad_maximum_fusion.2
  753.7 8.7 %select_maximum_fusion = f32[1,40,136,264]{3,2,1,0:T(8,128)} fusion(f32[1,40,4,256]{3,2,1,0:T(4,128)S(1)} %collective-permute-done.14, f32[1,40,4,256]{3,2,1,0:T(4,128)S(1)} %collective-permute-done.15, f32[1,4,128,256]{3,2,1,0:T(8,128)S(1)} %collective-permute-done.12, f32[1,32,128,256]{3,2,1,0:T(8,128)S(1)} %copy-done.2, ...), kind=kLoop, calls=%fused_computation.8 | loop fusion | flops 17233920 | bytes 11315200 | tf_op jit(solution)/shard_map/concatenate | solution.py:24
  762.3 65.5 %fusion.12 = f32[1,32,128,256]{3,2,1,0:T(8,128)} fusion(f32[1,32,128,256]{3,2,1,0:T(8,128)} %fusion.43, bf16[32,128,256]{2,1,0:T(8,128)(2,1)S(1)} %copy-done.5, bf16[32,128,256]{2,1,0:T(8,128)(2,1)} %get-tuple-element.6, f32[1,4,128,256]{3,2,1,0:T(8,128)S(1)} %collective-permute-done.13, f32[1,4,128,256]{3,2,1,0:T(8,128)S(1)} %collective-permute-done.12, ...), kind=kLoop, calls=%fused_computation.92 | loop fusion | flops 52428800 | bytes 95420416 | tf_op jit(solution)/shard_map/sub | solution.py:82
  (42 shorter events, 29.2 us)
Async XLA Ops:
  7.2 457.3 %all-reduce.7.cloned.1.call-start = ((), (), s32[]{:S(2)}) async-start(), calls=%async_computation | async-start | bytes 25165824 | tf_op jit(solution)/shard_map/psum | solution.py:12
  34.9 10.5 %collective-permute-start.1 = (f32[1,4,128,256]{3,2,1,0:T(8,128)S(1)}, f32[1,4,128,256]{3,2,1,0:T(8,128)S(1)}, u32[]{:S(2)}, u32[]{:S(2)}) collective-permute-start(f32[1,4,128,256]{3,2,1,0:T(8,128)S(1)} %get-tuple-element.38), channel_id=1, source_target_pairs={{0,2},{2,4},{4,6},{1,3},{3,5},{5,7},{8,10},{10,12},{12,14},{9,11},... | collective-permute-start | bytes 1572872 | tf_op jit(solution)/shard_map/ppermute | solution.py:20
  36.8 16.5 %collective-permute-start = (f32[1,4,128,256]{3,2,1,0:T(8,128)S(1)}, f32[1,4,128,256]{3,2,1,0:T(8,128)S(1)}, u32[]{:S(2)}, u32[]{:S(2)}) collective-permute-start(f32[1,4,128,256]{3,2,1,0:T(8,128)S(1)} %get-tuple-element.37), channel_id=1, source_target_pairs={{2,0},{4,2},{6,4},{3,1},{5,3},{7,5},{10,8},{12,10},{14,12},{11,9},... | collective-permute-start | bytes 1572872 | tf_op jit(solution)/shard_map/ppermute | solution.py:23
  46.3 12.3 %copy-start.6 = (f32[256]{0:T(256)S(1)}, f32[256]{0:T(256)}, u32[]{:S(2)}) copy-start(f32[256]{0:T(256)} %param.14) | copy-start | bytes 3076
  54.2 9.7 %copy-start.3 = (f32[1,40,128,256]{3,2,1,0:T(8,128)}, f32[1,40,128,256]{3,2,1,0:T(8,128)S(1)}, u32[]{:S(2)}) copy-start(f32[1,40,128,256]{3,2,1,0:T(8,128)S(1)} %get-tuple-element.40) | copy-start | bytes 15728644
  54.2 5.2 collective-permute-start.2
  56.7 7.2 collective-permute-start.3
  519.7 27.2 %copy-start = (f32[1,32,128,256]{3,2,1,0:T(8,128)}, f32[1,32,128,256]{3,2,1,0:T(8,128)S(1)}, u32[]{:S(2)}) copy-start(f32[1,32,128,256]{3,2,1,0:T(8,128)S(1)} %fusion.103) | copy-start | bytes 12582916
  519.8 8.6 %collective-permute-start.4 = (f32[1,4,128,256]{3,2,1,0:T(8,128)S(1)}, f32[1,4,128,256]{3,2,1,0:T(8,128)S(1)}, u32[]{:S(2)}, u32[]{:S(2)}) collective-permute-start(f32[1,4,128,256]{3,2,1,0:T(8,128)S(1)} %get-tuple-element.26), channel_id=1, source_target_pairs={{2,0},{4,2},{6,4},{3,1},{5,3},{7,5},{10,8},{12,10},{14,12},{11,9},... | collective-permute-start | bytes 1572872 | tf_op jit(solution)/shard_map/ppermute | solution.py:23
  521.8 10.5 %collective-permute-start.5 = (f32[1,4,128,256]{3,2,1,0:T(8,128)S(1)}, f32[1,4,128,256]{3,2,1,0:T(8,128)S(1)}, u32[]{:S(2)}, u32[]{:S(2)}) collective-permute-start(f32[1,4,128,256]{3,2,1,0:T(8,128)S(1)} %get-tuple-element.27), channel_id=1, source_target_pairs={{0,2},{2,4},{4,6},{1,3},{3,5},{5,7},{8,10},{10,12},{12,14},{9,11},... | collective-permute-start | bytes 1572872 | tf_op jit(solution)/shard_map/ppermute | solution.py:20
  532.3 5.3 collective-permute-start.6
  534.8 7.2 collective-permute-start.7
  546.9 8.7 %copy-start.4 = (bf16[32,128,256]{2,1,0:T(8,128)(2,1)S(1)}, bf16[32,128,256]{2,1,0:T(8,128)(2,1)}, u32[]{:S(2)}) copy-start(bf16[32,128,256]{2,1,0:T(8,128)(2,1)} %get-tuple-element.3) | copy-start | bytes 6291460
  621.9 23.8 %copy-start.1 = (f32[1,32,128,256]{3,2,1,0:T(8,128)S(1)}, f32[1,32,128,256]{3,2,1,0:T(8,128)}, u32[]{:S(2)}) copy-start(f32[1,32,128,256]{3,2,1,0:T(8,128)} %fusion.74) | copy-start | bytes 12582916
  623.3 8.7 %collective-permute-start.8 = (f32[1,4,128,256]{3,2,1,0:T(8,128)S(1)}, f32[1,4,128,256]{3,2,1,0:T(8,128)S(1)}, u32[]{:S(2)}, u32[]{:S(2)}) collective-permute-start(f32[1,4,128,256]{3,2,1,0:T(8,128)S(1)} %get-tuple-element.24), channel_id=1, source_target_pairs={{2,0},{4,2},{6,4},{3,1},{5,3},{7,5},{10,8},{12,10},{14,12},{11,9},... | collective-permute-start | bytes 1572872 | tf_op jit(solution)/shard_map/ppermute | solution.py:23
  625.4 10.5 %collective-permute-start.9 = (f32[1,4,128,256]{3,2,1,0:T(8,128)S(1)}, f32[1,4,128,256]{3,2,1,0:T(8,128)S(1)}, u32[]{:S(2)}, u32[]{:S(2)}) collective-permute-start(f32[1,4,128,256]{3,2,1,0:T(8,128)S(1)} %get-tuple-element.25), channel_id=1, source_target_pairs={{0,2},{2,4},{4,6},{1,3},{3,5},{5,7},{8,10},{10,12},{12,14},{9,11},... | collective-permute-start | bytes 1572872 | tf_op jit(solution)/shard_map/ppermute | solution.py:20
  637.0 4.3 collective-permute-start.10
  638.4 7.2 collective-permute-start.11
  725.0 23.8 %copy-start.2 = (f32[1,32,128,256]{3,2,1,0:T(8,128)S(1)}, f32[1,32,128,256]{3,2,1,0:T(8,128)}, u32[]{:S(2)}) copy-start(f32[1,32,128,256]{3,2,1,0:T(8,128)} %fusion.43) | copy-start | bytes 12582916
  726.5 8.7 %collective-permute-start.12 = (f32[1,4,128,256]{3,2,1,0:T(8,128)S(1)}, f32[1,4,128,256]{3,2,1,0:T(8,128)S(1)}, u32[]{:S(2)}, u32[]{:S(2)}) collective-permute-start(f32[1,4,128,256]{3,2,1,0:T(8,128)S(1)} %get-tuple-element.22), channel_id=1, source_target_pairs={{2,0},{4,2},{6,4},{3,1},{5,3},{7,5},{10,8},{12,10},{14,12},{11,9},... | collective-permute-start | bytes 1572872 | tf_op jit(solution)/shard_map/ppermute | solution.py:23
  728.5 10.5 %collective-permute-start.13 = (f32[1,4,128,256]{3,2,1,0:T(8,128)S(1)}, f32[1,4,128,256]{3,2,1,0:T(8,128)S(1)}, u32[]{:S(2)}, u32[]{:S(2)}) collective-permute-start(f32[1,4,128,256]{3,2,1,0:T(8,128)S(1)} %get-tuple-element.23), channel_id=1, source_target_pairs={{0,2},{2,4},{4,6},{1,3},{3,5},{5,7},{8,10},{10,12},{12,14},{9,11},... | collective-permute-start | bytes 1572872 | tf_op jit(solution)/shard_map/ppermute | solution.py:20
  740.1 4.3 collective-permute-start.14
  741.6 7.2 collective-permute-start.15
  753.7 8.7 %copy-start.5 = (bf16[32,128,256]{2,1,0:T(8,128)(2,1)S(1)}, bf16[32,128,256]{2,1,0:T(8,128)(2,1)}, u32[]{:S(2)}) copy-start(bf16[32,128,256]{2,1,0:T(8,128)(2,1)} %get-tuple-element.5) | copy-start | bytes 6291460
Sparse Core Ops, SparseCore 0:
  33.8 430.6 all-reduce.6
where the time goes:
time: 836 us; the launch traced here: 835 us
  waiting for transfers between devices  446 us (53%)
  other arithmetic  312 us (37%)
  starting transfers between devices  32.6 us (4%)
  between operations  30.1 us (4%)
  local copies, waits for them, and re-layouts  14.6 us (2%)
    psum x1, waiting for transfers between devices, spread(): return lax.psum(kept, axis)  395 us
    sub x4, other arithmetic, shards(): 2.0 * current - previous + courant[None] * laplace - scaled * source[None]  253 us
    concatenate x10, other arithmetic, with_halo(): block = jnp.concatenate([low, block, high], axis=dim)  48.7 us
    ppermute x8, waiting for transfers between devices, with_halo(): lax.ppermute(lax.slice_in_dim(block, block.shape[dim] - width, None, axis...  34 us
    ppermute x8, starting transfers between devices, with_halo(): lax.ppermute(lax.slice_in_dim(block, 0, width, axis=dim), axis, backward)  17.5 us
    ppermute x8, waiting for transfers between devices, with_halo(): lax.ppermute(lax.slice_in_dim(block, 0, width, axis=dim), axis, backward)  16.8 us
  transfers between devices with their start and end apart: 17, of which 16 were waited for; matrix products, arithmetic and copies ran while one was open for 2% of the time, Pallas kernels for 0%

commit v1 on v0

--- a/solution.py
+++ b/solution.py
@@ -9,7 +9,7 @@
 
 def spread(value, axis, source):
     kept = jnp.where(lax.axis_index(axis) == source, value, 0).astype(value.dtype)
-    return lax.psum(kept, axis)
+    return jnp.sum(lax.all_gather(kept, axis), axis=0)
 
 
 def with_halo(block, sides, width):

time: 836 us -> 1030 us (1.23)
  waiting for transfers between devices: 446 us -> 577 us
  other arithmetic: 312 us -> 365 us
    all_gather x0 -> x6, waiting for transfers between devices: none -> 540 us  [spread(): return jnp.sum(lax.all_gather(kept, axis), axis=0)]
    psum x1 -> x0, waiting for transfers between devices: 395 us -> none  [spread(): return lax.psum(kept, axis)]
    reduce_sum x0 -> x6, other arithmetic: none -> 39.7 us  [spread(): return jnp.sum(lax.all_gather(kept, axis), axis=0)]
    ppermute x8, waiting for transfers between devices: 34 us -> 20.7 us  [with_halo(): lax.ppermute(lax.slice_in_dim(block, block.shape[dim] - width, None, axis...]
  transfers between devices with their start and end apart: 17 -> 22, of which waited for: 16 -> 14; matrix products, arithmetic and copies ran while one was open for 2% -> 28% of each run, Pallas kernels for 0% -> 0%
where the time goes in v1:
time: 1030 us
  waiting for transfers between devices  577 us (56%)
  other arithmetic  365 us (35%)
  starting transfers between devices  41.3 us (4%)
  between operations  30.7 us (3%)
  local copies, waits for them, and re-layouts  14.6 us (1%)
    all_gather x6, waiting for transfers between devices, spread(): return jnp.sum(lax.all_gather(kept, axis), axis=0)  540 us
    sub x4, other arithmetic, shards(): 2.0 * current - previous + courant[None] * laplace - scaled * source[None]  255 us
    concatenate x10, other arithmetic, with_halo(): block = jnp.concatenate([low, block, high], axis=dim)  59 us
    reduce_sum x6, other arithmetic, spread(): return jnp.sum(lax.all_gather(kept, axis), axis=0)  39.7 us
    ppermute x8, starting transfers between devices, with_halo(): lax.ppermute(lax.slice_in_dim(block, 0, width, axis=dim), axis, backward)  27.2 us
    ppermute x8, waiting for transfers between devices, with_halo(): lax.ppermute(lax.slice_in_dim(block, block.shape[dim] - width, None, axis...  20.7 us
  transfers between devices with their start and end apart: 22, of which 14 were waited for; matrix products, arithmetic and copies ran while one was open for 28% of the time, Pallas kernels for 0%

profile of v1, /device:TPU:6, one launch (start us, length us, event | category | flops | bytes accessed | tf_op | source)
XLA Modules:
  0.0 1028.0 jit_solution(13175628013835229993)
XLA Ops:
  24.3 9.9 dynamic-slice_select_fusion
  43.8 4.9 collective-permute-done.1
  49.6 7.1 constant_dynamic-update-slice_fusion.1
  67.3 5.7 select_maximum_fusion.12
  73.0 112.2 %all-gather.11.cloned.1.call-done = bf16[4,32,128,256]{3,2,1,0:T(8,128)(2,1)} async-done(((bf16[1,32,128,256]{3,2,1,0:T(8,128)(2,1)}), bf16[4,32,128,256]{3,2,1,0:T(8,128)(2,1)}) %all-gather.11.cloned.1.call-update) | async-done | bytes 8388624 | tf_op jit(solution)/shard_map/all_gather | solution.py:12
  185.2 6.9 reduce_sum.84
  192.1 142.6 %all-gather.9.cloned.1.call-done = bf16[4,32,128,256]{3,2,1,0:T(8,128)(2,1)} async-done(((bf16[1,32,128,256]{3,2,1,0:T(8,128)(2,1)}), bf16[4,32,128,256]{3,2,1,0:T(8,128)(2,1)}) %all-gather.9.cloned.1.call-update) | async-done | bytes 8388624 | tf_op jit(solution)/shard_map/all_gather | solution.py:12
  334.7 6.9 reduce_sum.83
  341.6 142.5 %all-gather.7.cloned.1.call-done = bf16[4,32,128,256]{3,2,1,0:T(8,128)(2,1)} async-done(((bf16[1,32,128,256]{3,2,1,0:T(8,128)(2,1)}), bf16[4,32,128,256]{3,2,1,0:T(8,128)(2,1)}) %all-gather.7.cloned.1.call-update) | async-done | bytes 8388624 | tf_op jit(solution)/shard_map/all_gather | solution.py:12
  484.1 5.2 reduce_sum.82
  489.3 56.5 %fusion.103 = f32[1,32,128,256]{3,2,1,0:T(8,128)S(1)} fusion(f32[1,40,128,256]{3,2,1,0:T(8,128)} %copy-done.5, f32[1,40,4,256]{3,2,1,0:T(4,128)S(1)} %collective-permute-done.3, f32[1,40,4,256]{3,2,1,0:T(4,128)S(1)} %collective-permute-done.2, f32[1,40,136,264]{3,2,1,0:T(8,128)} %select_maximum_fusion.12, f32[1,36,128,256]{3,2,1,0:T(8,128)} %get-tuple-element.29, ...), kind=kLoop, calls=%fused_computation.183 | loop fusion | flops 52428800 | bytes 99942400 | tf_op jit(solution)/shard_map/sub | solution.py:82
  550.3 4.4 collective-permute-done.4
  560.7 5.1 collective-permute-start.6
  565.8 68.3 %all-gather.13.cloned.1.call-done = bf16[4,32,128,256]{3,2,1,0:T(8,128)(2,1)} async-done(((bf16[1,32,128,256]{3,2,1,0:T(8,128)(2,1)}), bf16[4,32,128,256]{3,2,1,0:T(8,128)(2,1)}) %all-gather.13.cloned.1.call-update) | async-done | bytes 8388624 | tf_op jit(solution)/shard_map/all_gather | solution.py:12
  634.0 6.9 reduce_sum.85
  641.0 11.3 %select_maximum_fusion.8 = f32[1,40,136,264]{3,2,1,0:T(8,128)} fusion(f32[1,40,4,256]{3,2,1,0:T(4,128)S(1)} %collective-permute-done.6, f32[1,40,4,256]{3,2,1,0:T(4,128)S(1)} %collective-permute-done.7, f32[1,4,128,256]{3,2,1,0:T(8,128)S(1)} %collective-permute-done.4, f32[1,32,128,256]{3,2,1,0:T(8,128)} %copy-done, ...), kind=kLoop, calls=%fused_computation.16 | loop fusion | flops 17233920 | bytes 11315200 | tf_op jit(solution)/shard_map/concatenate | solution.py:24
  652.3 4.8 pad_maximum_fusion
  657.1 66.1 %fusion.74 = f32[1,32,128,256]{3,2,1,0:T(8,128)} fusion(f32[1,32,128,256]{3,2,1,0:T(8,128)} %copy-done, f32[1,4,128,256]{3,2,1,0:T(8,128)S(1)} %collective-permute-done.5, f32[1,4,128,256]{3,2,1,0:T(8,128)S(1)} %collective-permute-done.4, f32[1,40,136,264]{3,2,1,0:T(8,128)} %select_maximum_fusion.8, f32[1,40,132,256]{3,2,1,0:T(8,128)} %get-tuple-element.11, ...), kind=kLoop, calls=%fused_computation.154 | loop fusion | flops 52428800 | bytes 95420416 | tf_op jit(solution)/shard_map/sub | solution.py:82
  728.8 4.4 collective-permute-done.8
  740.2 4.7 collective-permute-start.10
  744.9 38.5 %all-gather.15.cloned.1.call-done = bf16[4,32,128,256]{3,2,1,0:T(8,128)(2,1)} async-done(((bf16[1,32,128,256]{3,2,1,0:T(8,128)(2,1)}), bf16[4,32,128,256]{3,2,1,0:T(8,128)(2,1)}) %all-gather.15.cloned.1.call-update) | async-done | bytes 8388624 | tf_op jit(solution)/shard_map/all_gather | solution.py:12
  783.3 6.9 reduce_sum.86
  790.2 8.7 pad_maximum_fusion.1
  799.1 8.7 select_maximum_fusion.4
  807.8 67.4 %fusion.43 = f32[1,32,128,256]{3,2,1,0:T(8,128)} fusion(f32[1,32,128,256]{3,2,1,0:T(8,128)} %fusion.74, f32[1,4,128,256]{3,2,1,0:T(8,128)S(1)} %collective-permute-done.9, f32[1,4,128,256]{3,2,1,0:T(8,128)S(1)} %collective-permute-done.8, f32[1,40,136,264]{3,2,1,0:T(8,128)} %select_maximum_fusion.4, f32[1,40,132,256]{3,2,1,0:T(8,128)} %get-tuple-element.7, ...), kind=kLoop, calls=%fused_computation.123 | loop fusion | flops 52428800 | bytes 95420416 | tf_op jit(solution)/shard_map/sub | solution.py:82
  880.9 4.6 collective-permute-done.12
  891.8 4.8 collective-permute-start.14
  896.6 36.1 %all-gather.17.cloned.1.call-done = bf16[4,32,128,256]{3,2,1,0:T(8,128)(2,1)} async-done(((bf16[1,32,128,256]{3,2,1,0:T(8,128)(2,1)}), bf16[4,32,128,256]{3,2,1,0:T(8,128)(2,1)}) %all-gather.17.cloned.1.call-update) | async-done | bytes 8388624 | tf_op jit(solution)/shard_map/all_gather | solution.py:12
  932.7 6.9 reduce_sum.87
  939.6 11.2 %select_maximum_fusion = f32[1,40,136,264]{3,2,1,0:T(8,128)} fusion(f32[1,40,4,256]{3,2,1,0:T(4,128)S(1)} %collective-permute-done.14, f32[1,40,4,256]{3,2,1,0:T(4,128)S(1)} %collective-permute-done.15, f32[1,4,128,256]{3,2,1,0:T(8,128)S(1)} %collective-permute-done.12, f32[1,32,128,256]{3,2,1,0:T(8,128)} %fusion.43, ...), kind=kLoop, calls=%fused_computation.8 | loop fusion | flops 17233920 | bytes 11315200 | tf_op jit(solution)/shard_map/concatenate | solution.py:24
  950.7 4.8 pad_maximum_fusion.2
  955.6 65.3 %fusion.12 = f32[1,32,128,256]{3,2,1,0:T(8,128)} fusion(f32[1,32,128,256]{3,2,1,0:T(8,128)} %fusion.43, f32[1,4,128,256]{3,2,1,0:T(8,128)S(1)} %collective-permute-done.13, f32[1,4,128,256]{3,2,1,0:T(8,128)S(1)} %collective-permute-done.12, f32[1,40,136,264]{3,2,1,0:T(8,128)} %select_maximum_fusion, f32[1,40,132,256]{3,2,1,0:T(8,128)} %get-tuple-element.3, ...), kind=kLoop, calls=%fused_computation.92 | loop fusion | flops 52428800 | bytes 95420416 | tf_op jit(solution)/shard_map/sub | solution.py:82
  (63 shorter events, 56.8 us)
Async XLA Ops:
  7.2 178.0 %all-gather.11.cloned.1.call-start = ((), (), s32[]{:S(2)}) async-start(), calls=%async_computation.2 | async-start | bytes 10485760 | tf_op jit(solution)/shard_map/all_gather | solution.py:12
  34.2 300.4 %all-gather.9.cloned.1.call-start = ((), (), s32[]{:S(2)}) async-start(), calls=%async_computation.1 | async-start | bytes 10485760 | tf_op jit(solution)/shard_map/all_gather | solution.py:12
  35.0 449.2 %all-gather.7.cloned.1.call-start = ((), (), s32[]{:S(2)}) async-start(), calls=%async_computation | async-start | bytes 10485760 | tf_op jit(solution)/shard_map/all_gather | solution.py:12
  35.7 598.3 %all-gather.13.cloned.1.call-start = ((), (), s32[]{:S(2)}) async-start(), calls=%async_computation.3 | async-start | bytes 10485760 | tf_op jit(solution)/shard_map/all_gather | solution.py:12
  36.3 747.1 %all-gather.15.cloned.1.call-start = ((), (), s32[]{:S(2)}) async-start(), calls=%async_computation.4 | async-start | bytes 10485760 | tf_op jit(solution)/shard_map/all_gather | solution.py:12
  36.9 895.8 %all-gather.17.cloned.1.call-start = ((), (), s32[]{:S(2)}) async-start(), calls=%async_computation.5 | async-start | bytes 10485760 | tf_op jit(solution)/shard_map/all_gather | solution.py:12
  38.2 10.5 %collective-permute-start.1 = (f32[1,4,128,256]{3,2,1,0:T(8,128)S(1)}, f32[1,4,128,256]{3,2,1,0:T(8,128)S(1)}, u32[]{:S(2)}, u32[]{:S(2)}) collective-permute-start(f32[1,4,128,256]{3,2,1,0:T(8,128)S(1)} %get-tuple-element.32), channel_id=1, source_target_pairs={{0,2},{2,4},{4,6},{1,3},{3,5},{5,7},{8,10},{10,12},{12,14},{9,11},... | collective-permute-start | bytes 1572872 | tf_op jit(solution)/shard_map/ppermute | solution.py:20
  40.1 16.6 %collective-permute-start = (f32[1,4,128,256]{3,2,1,0:T(8,128)S(1)}, f32[1,4,128,256]{3,2,1,0:T(8,128)S(1)}, u32[]{:S(2)}, u32[]{:S(2)}) collective-permute-start(f32[1,4,128,256]{3,2,1,0:T(8,128)S(1)} %get-tuple-element.31), channel_id=1, source_target_pairs={{2,0},{4,2},{6,4},{3,1},{5,3},{7,5},{10,8},{12,10},{14,12},{11,9},... | collective-permute-start | bytes 1572872 | tf_op jit(solution)/shard_map/ppermute | solution.py:23
  49.6 12.8 %copy-start.6 = (f32[256]{0:T(256)S(1)}, f32[256]{0:T(256)}, u32[]{:S(2)}) copy-start(f32[256]{0:T(256)} %param.14) | copy-start | bytes 3076
  57.6 9.7 copy-start.5
  57.7 5.4 collective-permute-start.2
  60.1 7.2 collective-permute-start.3
  545.8 12.7 %copy-start = (f32[1,32,128,256]{3,2,1,0:T(8,128)}, f32[1,32,128,256]{3,2,1,0:T(8,128)S(1)}, u32[]{:S(2)}) copy-start(f32[1,32,128,256]{3,2,1,0:T(8,128)S(1)} %fusion.103) | copy-start | bytes 12582916
  545.9 8.8 collective-permute-start.4
  548.1 10.5 %collective-permute-start.5 = (f32[1,4,128,256]{3,2,1,0:T(8,128)S(1)}, f32[1,4,128,256]{3,2,1,0:T(8,128)S(1)}, u32[]{:S(2)}, u32[]{:S(2)}) collective-permute-start(f32[1,4,128,256]{3,2,1,0:T(8,128)S(1)} %get-tuple-element.27), channel_id=1, source_target_pairs={{0,2},{2,4},{4,6},{1,3},{3,5},{5,7},{8,10},{10,12},{12,14},{9,11},... | collective-permute-start | bytes 1572872 | tf_op jit(solution)/shard_map/ppermute | solution.py:20
  559.4 81.6 %collective-permute-start.7 = (f32[1,40,4,256]{3,2,1,0:T(4,128)}, f32[1,40,4,256]{3,2,1,0:T(4,128)S(1)}, u32[]{:S(2)}, u32[]{:S(2)}) collective-permute-start(f32[1,40,4,256]{3,2,1,0:T(4,128)} %get-tuple-element.12), channel_id=1, source_target_pairs={{0,1},{2,3},{4,5},{6,7},{8,9},{10,11},{12,13},{14,15},{16,17},{18,... | collective-permute-start | bytes 491528 | tf_op jit(solution)/shard_map/ppermute | solution.py:20
  560.7 80.3 %collective-permute-start.6 = (f32[1,40,4,256]{3,2,1,0:T(4,128)}, f32[1,40,4,256]{3,2,1,0:T(4,128)S(1)}, u32[]{:S(2)}, u32[]{:S(2)}) collective-permute-start(f32[1,40,4,256]{3,2,1,0:T(4,128)} %get-tuple-element.13), channel_id=1, source_target_pairs={{1,0},{3,2},{5,4},{7,6},{9,8},{11,10},{13,12},{15,14},{17,16},{19,... | collective-permute-start | bytes 491528 | tf_op jit(solution)/shard_map/ppermute | solution.py:23
  641.0 11.3 %copy-start.1 = (f32[1,32,128,256]{3,2,1,0:T(8,128)S(1)}, f32[1,32,128,256]{3,2,1,0:T(8,128)}, u32[]{:S(2)}) copy-start(f32[1,32,128,256]{3,2,1,0:T(8,128)} %copy-done) | copy-start | bytes 12582916
  724.4 8.8 collective-permute-start.8
  726.6 10.5 %collective-permute-start.9 = (f32[1,4,128,256]{3,2,1,0:T(8,128)S(1)}, f32[1,4,128,256]{3,2,1,0:T(8,128)S(1)}, u32[]{:S(2)}, u32[]{:S(2)}) collective-permute-start(f32[1,4,128,256]{3,2,1,0:T(8,128)S(1)} %get-tuple-element.25), channel_id=1, source_target_pairs={{0,2},{2,4},{4,6},{1,3},{3,5},{5,7},{8,10},{10,12},{12,14},{9,11},... | collective-permute-start | bytes 1572872 | tf_op jit(solution)/shard_map/ppermute | solution.py:20
  738.9 51.4 %collective-permute-start.11 = (f32[1,40,4,256]{3,2,1,0:T(4,128)}, f32[1,40,4,256]{3,2,1,0:T(4,128)S(1)}, u32[]{:S(2)}, u32[]{:S(2)}) collective-permute-start(f32[1,40,4,256]{3,2,1,0:T(4,128)} %get-tuple-element.8), channel_id=1, source_target_pairs={{0,1},{2,3},{4,5},{6,7},{8,9},{10,11},{12,13},{14,15},{16,17},{18,... | collective-permute-start | bytes 491528 | tf_op jit(solution)/shard_map/ppermute | solution.py:20
  740.2 50.1 %collective-permute-start.10 = (f32[1,40,4,256]{3,2,1,0:T(4,128)}, f32[1,40,4,256]{3,2,1,0:T(4,128)S(1)}, u32[]{:S(2)}, u32[]{:S(2)}) collective-permute-start(f32[1,40,4,256]{3,2,1,0:T(4,128)} %get-tuple-element.9), channel_id=1, source_target_pairs={{1,0},{3,2},{5,4},{7,6},{9,8},{11,10},{13,12},{15,14},{17,16},{19,... | collective-permute-start | bytes 491528 | tf_op jit(solution)/shard_map/ppermute | solution.py:23
  790.2 8.9 copy-start.2
  876.6 9.0 collective-permute-start.12
  878.9 10.5 %collective-permute-start.13 = (f32[1,4,128,256]{3,2,1,0:T(8,128)S(1)}, f32[1,4,128,256]{3,2,1,0:T(8,128)S(1)}, u32[]{:S(2)}, u32[]{:S(2)}) collective-permute-start(f32[1,4,128,256]{3,2,1,0:T(8,128)S(1)} %get-tuple-element.23), channel_id=1, source_target_pairs={{0,2},{2,4},{4,6},{1,3},{3,5},{5,7},{8,10},{10,12},{12,14},{9,11},... | collective-permute-start | bytes 1572872 | tf_op jit(solution)/shard_map/ppermute | solution.py:20
  890.5 49.1 %collective-permute-start.15 = (f32[1,40,4,256]{3,2,1,0:T(4,128)S(1)}, f32[1,40,4,256]{3,2,1,0:T(4,128)S(1)}, u32[]{:S(2)}, u32[]{:S(2)}) collective-permute-start(f32[1,40,4,256]{3,2,1,0:T(4,128)S(1)} %get-tuple-element.4), channel_id=1, source_target_pairs={{0,1},{2,3},{4,5},{6,7},{8,9},{10,11},{12,13},{14,15},{16,17},{18,... | collective-permute-start | bytes 491528 | tf_op jit(solution)/shard_map/ppermute | solution.py:20
  891.8 47.8 %collective-permute-start.14 = (f32[1,40,4,256]{3,2,1,0:T(4,128)S(1)}, f32[1,40,4,256]{3,2,1,0:T(4,128)S(1)}, u32[]{:S(2)}, u32[]{:S(2)}) collective-permute-start(f32[1,40,4,256]{3,2,1,0:T(4,128)S(1)} %get-tuple-element.5), channel_id=1, source_target_pairs={{1,0},{3,2},{5,4},{7,6},{9,8},{11,10},{13,12},{15,14},{17,16},{19,... | collective-permute-start | bytes 491528 | tf_op jit(solution)/shard_map/ppermute | solution.py:23
  939.5 11.2 %copy-start.3 = (f32[1,32,128,256]{3,2,1,0:T(8,128)S(1)}, f32[1,32,128,256]{3,2,1,0:T(8,128)}, u32[]{:S(2)}) copy-start(f32[1,32,128,256]{3,2,1,0:T(8,128)} %fusion.43) | copy-start | bytes 12582916
  950.7 4.8 copy-start.4
Sparse Core Ops, SparseCore 0:
  34.3 150.8 all-gather.10
  186.8 147.8 all-gather.8
  336.2 147.8 all-gather.6
  486.1 147.8 all-gather.12
  635.4 147.8 all-gather.14
  784.8 147.8 all-gather.16
